TPU v7x, 32 devices: a whole 2x2x4 slice. The times are simulated.
32 devices in a mesh: lat: 8 (over z, y), lon: 4 (over x, core).
Axes of the slice: x: 2, y: 2, z: 4, core: 2. Of those that a mesh axis runs over, the one named last changes fastest.
Arguments:
- pair_table: int32 [640], replicated, may hold values from 0 to 639, each once
- spectral: bfloat16 [640, 384, 1408], P('lat', 'lon'), may hold values from -0.071777344 to 0.071777344
- lat_basis: bfloat16 [640, 32, 1408], P('lat'), may hold values from -0.15625 to 0.15625
- in_weight: bfloat16 [192, 512], replicated, may hold values from -0.4375 to 0.4375
- in_bias: float32 [512], replicated, may hold values from -3 to 3
- out_weight: bfloat16 [512, 192], replicated, may hold values from -0.25 to 0.25
- out_bias: float32 [192], replicated, may hold values from -3 to 3
- cotangent: bfloat16 [64, 192, 2560], P('lat', None, 'lon'), may hold values from -0.08984375 to 0.08984375
Outputs:
- tendency: bfloat16 [64, 192, 2560], P('lat', None, 'lon')
- spectral_grad: bfloat16 [640, 384, 1408], P('lat', 'lon')
- in_weight_grad: float32 [192, 512], replicated
- in_bias_grad: float32 [512], replicated
- out_weight_grad: float32 [512, 192], replicated
- out_bias_grad: float32 [192], replicated
Inputs may be any that keep to these rules, and one draw needn't show every extreme that they name: `pair_table`: each pair number appears exactly once.
All inputs are finite; a program needn't handle non-finite values.
Results may differ from a plain program's by a relative error of at most 0.015.
Values may be sent and summed in bfloat16 or wider, within the bound.
No kernel may reach another device: no remote copies, remote signals or barrier semaphores. Data moves between devices by JAX's collectives and lax.ppermute only.
A program may use at most 256 MiB of HBM per device.

v0:
```python
import math
import jax
import jax.numpy as jnp
from jax import lax
from jax.sharding import PartitionSpec as P

TRUNC = 1279


def pair_masks(pair_ids, length):
    first_len = TRUNC + 1 - pair_ids
    position = jnp.arange(length, dtype=jnp.int32)[None, :]
    lower_part = position < first_len[:, None]
    upper_part = jnp.logical_and(position >= first_len[:, None], position < TRUNC + 2)
    offset = jnp.where(lower_part, position, position - first_len[:, None])
    parity = jnp.where(offset % 2 == 0, 1.0, -1.0).astype(jnp.float32)
    return (lower_part, upper_part, parity, first_len)


def wave_numbers(pair_ids):
    both = jnp.stack([pair_ids, TRUNC - pair_ids], axis=1)
    return both.reshape(-1)


def fourier_table(numbers, lon_total):
    step = 128 if lon_total % 128 == 0 else 1
    coarse = jnp.arange(lon_total // step, dtype=jnp.int32) * step
    fine = jnp.arange(step, dtype=jnp.int32)
    scale = 2.0 * math.pi / lon_total

    def angles(offsets):
        phase = numbers[:, None] * offsets[None, :] % lon_total
        angle = phase.astype(jnp.float32) * scale
        return (jnp.cos(angle), jnp.sin(angle))

    cos_a, sin_a = angles(coarse)
    cos_b, sin_b = angles(fine)
    cos_t = cos_a[:, :, None] * cos_b[:, None, :] - sin_a[:, :, None] * sin_b[:, None, :]
    sin_t = sin_a[:, :, None] * cos_b[:, None, :] + cos_a[:, :, None] * sin_b[:, None, :]
    count = numbers.shape[0]
    factor = jnp.where(numbers == 0, 1.0, 2.0).astype(jnp.float32)[:, None]
    return jnp.stack(
        [factor * cos_t.reshape(count, lon_total), -factor * sin_t.reshape(count, lon_total)],
        axis=1,
    ).astype(jnp.bfloat16)


def per_device(
    pair_table, spectral, lat_basis, in_weight, in_bias, out_weight, out_bias, cotangent
):
    pair_dev = spectral.shape[0]
    width_local = spectral.shape[1]
    lat_half = lat_basis.shape[1]
    band_rows = cotangent.shape[0]
    block_cols = cotangent.shape[2]
    lon_total = block_cols * lax.axis_size("lon")
    first_row = lax.axis_index("lat") * pair_dev
    local_ids = lax.dynamic_slice_in_dim(pair_table, first_row, pair_dev)
    lower_part, upper_part, parity, first_len = pair_masks(local_ids, spectral.shape[2])
    rows = jnp.concatenate([lat_basis, lat_basis * parity[:, None, :].astype(jnp.bfloat16)], axis=1)
    zero = jnp.zeros_like(rows)
    basis = jnp.stack(
        [
            jnp.where(lower_part[:, None, :], rows, zero),
            jnp.where(upper_part[:, None, :], rows, zero),
        ],
        axis=1,
    )
    lat_window = 2 * lat_half
    raw_waves = jnp.einsum(
        "pqlj,pkj->pqlk", basis, spectral, preferred_element_type=jnp.float32
    ).astype(jnp.bfloat16)
    waves = jnp.concatenate(
        [raw_waves[:, :, :lat_half], jnp.flip(raw_waves[:, :, lat_half:], axis=2)], axis=2
    )
    flat_waves = waves.reshape(2 * pair_dev, lat_window * width_local)
    band_waves = lax.all_to_all(flat_waves, "lat", split_axis=1, concat_axis=0, tiled=True)
    wave_count = band_waves.shape[0]
    coeff_grid = band_waves.reshape(wave_count, band_rows, width_local // 2, 2)
    numbers = wave_numbers(pair_table)
    full_table = fourier_table(numbers, lon_total)
    all_columns = jnp.einsum(
        "glkc,gcn->lkn", coeff_grid, full_table, preferred_element_type=jnp.float32
    ).astype(jnp.bfloat16)
    grid = lax.all_to_all(all_columns, "lon", split_axis=2, concat_axis=1, tiled=True)
    pre_act = (
        jnp.einsum("lkc,kh->lch", grid, in_weight, preferred_element_type=jnp.float32) + in_bias
    )
    activated, gelu_back = jax.vjp(jax.nn.gelu, pre_act)
    hidden = activated.astype(jnp.bfloat16)
    tendency = (
        jnp.einsum("lch,hk->lkc", hidden, out_weight, preferred_element_type=jnp.float32)
        + out_bias[None, :, None]
    ).astype(jnp.bfloat16)
    out_weight_part = jnp.einsum(
        "lch,lkc->kh", hidden, cotangent, preferred_element_type=jnp.float32
    )
    out_bias_part = jnp.sum(cotangent.astype(jnp.float32), axis=(0, 2))
    hidden_grad = jnp.einsum(
        "lkc,hk->lch", cotangent, out_weight, preferred_element_type=jnp.float32
    )
    pre_grad = gelu_back(hidden_grad)[0].astype(jnp.bfloat16)
    in_weight_part = jnp.einsum("lkc,lch->kh", grid, pre_grad, preferred_element_type=jnp.float32)
    in_bias_part = jnp.sum(pre_grad.astype(jnp.float32), axis=(0, 1))
    grid_grad = jnp.einsum(
        "lch,kh->lkc", pre_grad, in_weight, preferred_element_type=jnp.float32
    ).astype(jnp.bfloat16)
    channels, hid = in_weight.shape
    width = max(hid, channels)

    def widen(v):
        return jnp.pad(v, ((0, 0), (0, width - v.shape[1])))

    stacked = jnp.concatenate(
        [
            widen(in_weight_part),
            widen(out_weight_part),
            widen(in_bias_part[None, :]),
            widen(out_bias_part[None, :]),
        ],
        axis=0,
    )
    summed = lax.psum(stacked, ("lat", "lon"))
    in_weight_grad = summed[:channels, :hid]
    out_weight_grad = summed[channels : 2 * channels, :hid].T
    in_bias_grad = summed[2 * channels, :hid]
    out_bias_grad = summed[2 * channels + 1, :channels]
    level_rows = lax.all_to_all(grid_grad, "lon", split_axis=1, concat_axis=2, tiled=True)
    wave_grad = jnp.einsum(
        "gcn,lkn->glkc", full_table, level_rows, preferred_element_type=jnp.float32
    ).astype(jnp.bfloat16)
    flat_grad = wave_grad.reshape(wave_count, band_rows * width_local)
    pair_grad = lax.all_to_all(flat_grad, "lat", split_axis=0, concat_axis=1, tiled=True)
    pair_grad = pair_grad.reshape(pair_dev, 2, lat_window, width_local)
    pair_grad = jnp.concatenate(
        [pair_grad[:, :, :lat_half], jnp.flip(pair_grad[:, :, lat_half:], axis=2)], axis=2
    )
    spectral_grad = jnp.einsum(
        "pqlk,pqlj->pkj", pair_grad, basis, preferred_element_type=jnp.float32
    ).astype(jnp.bfloat16)
    return (tendency, spectral_grad, in_weight_grad, in_bias_grad, out_weight_grad, out_bias_grad)


def solution(mesh):
    placed = (
        P(),
        P("lat", "lon", None),
        P("lat", None, None),
        P(),
        P(),
        P(),
        P(),
        P("lat", None, "lon"),
    )
    return jax.shard_map(
        per_device,
        mesh=mesh,
        in_specs=placed,
        out_specs=(P("lat", None, "lon"), P("lat", "lon", None), P(), P(), P(), P()),
        check_vma=False,
    )
```

profile of v0, /device:TPU:1, one launch (start us, length us, event | category | flops | bytes accessed | tf_op | source)
XLA Modules:
  0.0 477.1 jit_solution(11046358141665475062)
XLA Ops:
  7.2 0.0 copy-start
  7.2 0.8 dynamic-slice_subtract_fusion
  8.0 0.3 select_convert_fusion
  8.3 0.0 slice-start
  8.4 0.2 iota_compare_fusion.2
  8.6 0.0 slice-start.1
  8.6 7.1 %multiply_bitcast_fusion = bf16[80,1,32,1408]{3,2,1,0:T(8,128)(2,1)} fusion(bf16[80,32,1408]{2,1,0:T(8,128)(2,1)} %param.10, bf16[80,1408]{1,0:T(8,128)(2,1)S(1)} %select_convert_fusion), kind=kLoop, calls=%fused_computation.25 | loop fusion | flops 3604480 | bytes 14643200 | tf_op jit(solution)/shard_map/concatenate | solution.py:60
  15.7 14.2 %broadcast_select_fusion.1 = (bf16[80,1,64,1408]{3,2,1,0:T(8,128)(2,1)}, bf16[80,1,64,1408]{3,2,1,0:T(8,128)(2,1)}) fusion(pred[80,1408]{1,0:T(8,128)(4,1)S(1)} %get-tuple-element.22, bf16[80,1,32,1408]{3,2,1,0:T(8,128)(2,1)} %multiply_bitcast_fusion, bf16[80,1,32,1408]{3,2,1,0:T(8,128)(2,1)S(1)} %bitcast.97, pred[80,1408]{1,0:T(8,128)(4,1)S(1)} %get-tuple-element.23), kind=kLoop, calls=%fused_computation.8 | loop fusion | flops 43253760 | bytes 43479040 | tf_op jit(solution)/shard_map/jit(_where)/select_n | solution.py:64
  29.8 20.0 %fusion.18 = bf16[80,2,64,96]{3,2,1,0:T(8,128)(2,1)} fusion(bf16[80,96,1408]{2,1,0:T(8,128)(2,1)} %param.9, bf16[80,1,64,1408]{3,2,1,0:T(8,128)(2,1)} %get-tuple-element.7, bf16[80,1,64,1408]{3,2,1,0:T(8,128)(2,1)} %get-tuple-element.6), kind=kOutput, calls=%fused_computation.36 | convolution fusion | flops 2783641600 | bytes 52428800 | tf_op jit(solution)/shard_map/pqlj,pkj->pqlk/dot_general | solution.py:70
  49.8 3.4 fusion.52
  53.2 2.6 rev.7
  55.7 2.5 pad_maximum_fusion.4
  58.3 0.0 copy-start.6
  58.3 3.1 all_to_all.50
  61.4 3.2 copy.25
  64.6 6.9 %all-to-all-start = ((bf16[160,8,768]{2,0,1:T(8,128)(2,1)}), bf16[160,8,768]{2,0,1:T(8,128)(2,1)S(1)}, u32[]{:S(2)}, u32[]{:S(2)}) async-start(bf16[160,8,768]{2,0,1:T(8,128)(2,1)} %copy.25), calls=%async_computation | async-start | bytes 3932160 | tf_op jit(solution)/shard_map/all_to_all | solution.py:77
  71.6 0.2 copy.27
  71.8 0.2 reshape.455
  72.0 2.6 fusion.29
  74.7 1.3 fusion.44
  75.9 13.6 %multiply_subtract_fusion = (f32[1280,20,128]{0,2,1:T(8,128)}, f32[1280,20,128]{0,2,1:T(8,128)}) fusion(f32[1280,128]{0,1:T(8,128)S(1)} %get-tuple-element.21, f32[1280,20]{0,1:T(8,128)} %get-tuple-element.17, f32[1280,128]{0,1:T(8,128)S(1)} %get-tuple-element.20, f32[1280,20]{0,1:T(8,128)} %get-tuple-element.16), kind=kLoop, calls=%fused_computation.13 | loop fusion | flops 19660800 | bytes 27729920 | tf_op jit(solution)/shard_map/sub | solution.py:38
  89.6 14.0 %copy.29 = f32[1280,1,2560]{2,0,1:T(8,128)} copy(f32[1280,1,2560]{0,2,1:T(8,128)} %bitcast.94) | data formatting | bytes 26214400 | tf_op jit(solution)/shard_map/add | solution.py:39
  103.6 14.0 %copy.28 = f32[1280,1,2560]{2,0,1:T(8,128)} copy(f32[1280,1,2560]{0,2,1:T(8,128)} %bitcast.93) | data formatting | bytes 26214400 | tf_op jit(solution)/shard_map/sub | solution.py:38
  117.5 13.9 %multiply_convert_fusion = (bf16[1280,1,2560]{2,0,1:T(8,128)(2,1)}, bf16[1280,1,2560]{2,0,1:T(8,128)(2,1)}) fusion(f32[1280,1,2560]{2,0,1:T(8,128)} %copy.29, f32[1280]{0:T(1024)S(1)} %get-tuple-element.19, f32[1280,1,2560]{2,0,1:T(8,128)} %copy.28, f32[1280]{0:T(1024)S(1)} %get-tuple-element.18), kind=kLoop, calls=%fused_computation.10 | loop fusion | flops 13107200 | bytes 39331840 | tf_op jit(solution)/shard_map/convert.1
  131.5 1.3 copy-done.1
  132.7 4.1 copy.26
  136.8 5.2 %reshape.454 = bf16[1280,8,48,2]{0,3,2,1:T(2,128)(2,1)} reshape(bf16[8,160,768]{1,0,2:T(8,128)(2,1)S(1)} %copy.26) | data formatting | bytes 3932160 | tf_op jit(solution)/shard_map/reshape | solution.py:79
  142.1 8.9 %fusion.12 = bf16[8,48,2560]{2,1,0:T(8,128)(2,1)S(1)} fusion(bf16[1280,1,2560]{2,0,1:T(8,128)(2,1)} %get-tuple-element.28, bf16[1280,1,2560]{2,0,1:T(8,128)(2,1)} %get-tuple-element.29, bf16[1280,8,48,2]{0,3,2,1:T(2,128)(2,1)} %reshape.454), kind=kOutput, calls=%fused_computation.27 | convolution fusion | flops 5040701440 | bytes 17039360 | tf_op jit(solution)/shard_map/glkc,gcn->lkn/dot_general | solution.py:82
  151.0 5.4 %copy.31 = bf16[8,48,2560]{1,0,2:T(8,128)(2,1)} copy(bf16[8,48,2560]{2,1,0:T(8,128)(2,1)S(1)} %fusion.12) | data formatting | bytes 3932160 | tf_op jit(solution)/shard_map/convert_element_type | solution.py:84
  156.4 8.8 %reshape.467 = bf16[4,2,122880]{2,1,0:T(2,128)(2,1)S(1)} reshape(bf16[2560,8,48]{2,1,0:T(8,128)(2,1)} %bitcast.98) | data formatting | bytes 3932160
  165.3 27.4 %all_to_all.68 = bf16[4,2,122880]{2,1,0:T(2,128)(2,1)} all-to-all(bf16[4,2,122880]{2,1,0:T(2,128)(2,1)S(1)} %reshape.467), channel_id=1, replica_groups=mesh['lat'=8,'lon'=4] {'lon'}, dimensions={0} | all-to-all | bytes 3932160 | tf_op jit(solution)/shard_map/all_to_all | solution.py:85
  192.7 7.1 %reshape.468 = bf16[2560,8,48]{2,1,0:T(8,128)(2,1)} reshape(bf16[4,2,122880]{2,1,0:T(2,128)(2,1)} %all_to_all.68) | data formatting | bytes 3932160
  199.8 5.7 %copy.32 = bf16[8,48,4,640]{3,1,2,0:T(8,128)(2,1)S(1)} copy(bf16[8,48,4,640]{1,0,3,2:T(8,128)(2,1)} %bitcast.99) | data formatting | bytes 3932160 | tf_op jit(solution)/shard_map/all_to_all | solution.py:85
  205.5 0.0 copy-start.3
  205.5 0.0 copy-start.7
  205.5 5.5 %multiply_convert_fusion.2 = (bf16[8,640,512]{2,1,0:T(8,128)(2,1)}, f32[8,640,512]{2,1,0:T(8,128)S(1)}) fusion(f32[512]{0:T(512)S(1)} %copy-done.8, bf16[8,192,640]{2,1,0:T(8,128)(2,1)S(1)} %bitcast.104, bf16[192,512]{1,0:T(8,128)(2,1)S(1)} %copy-done), kind=kOutput, calls=%fused_computation.22 | convolution fusion | flops 1032847360 | bytes 17893376 | tf_op jit(solution)/shard_map/lkc,kh->lch/dot_general | solution.py:87
  211.0 8.7 %convert_reduce_fusion = (f32[512]{0:T(512)S(1)}, bf16[8,640,512]{2,1,0:T(8,128)(2,1)S(1)}) fusion(f32[8,640,512]{2,1,0:T(8,128)S(1)} %get-tuple-element.25, f32[512]{0:T(512)S(1)} %copy-done.8, bf16[8,192,640]{2,1,0:T(8,128)(2,1)S(1)} %copy-done.3, bf16[512,192]{0,1:T(8,128)(2,1)S(1)} %copy-done.7), kind=kOutput, calls=%fused_computation.21 | convolution fusion | flops 1066925568 | bytes 17895424 | tf_op jit(solution)/shard_map/lkc,hk->lch/dot_general | solution.py:99
  219.7 1.9 convert_bitcast_fusion
  221.6 1.1 copy.33
  222.7 26.9 %all_to_all.69 = bf16[8,192,640]{2,0,1:T(8,128)(2,1)S(1)} all-to-all(bf16[8,192,640]{2,0,1:T(8,128)(2,1)S(1)} %copy.33), channel_id=1, replica_groups=mesh['lat'=8,'lon'=4] {'lon'}, dimensions={1} | all-to-all | bytes 3932160 | tf_op jit(solution)/shard_map/all_to_all | solution.py:128
  249.7 1.5 copy.45
  251.2 2.2 reshape.462
  253.4 9.0 %fusion.14 = bf16[1280,8,48,2]{0,2,3,1:T(8,128)(2,1)S(1)} fusion(bf16[1280,1,2560]{2,0,1:T(8,128)(2,1)} %get-tuple-element.28, bf16[1280,1,2560]{2,0,1:T(8,128)(2,1)} %get-tuple-element.29, bf16[8,48,2560,1]{2,1,0,3:T(8,128)(2,1)} %reshape.462), kind=kOutput, calls=%fused_computation.31 | convolution fusion | flops 5060362240 | bytes 17039360 | tf_op jit(solution)/shard_map/gcn,lkn->glkc/dot_general | solution.py:129
  262.4 2.8 copy.35
  265.2 6.4 %all_to_all.61 = bf16[8,160,768]{1,0,2:T(8,128)(2,1)S(1)} reshape(bf16[1280,8,48,2]{0,3,2,1:T(2,128)(2,1)} %copy.35) | data formatting | bytes 3932160 | tf_op jit(solution)/shard_map/all_to_all | solution.py:133
  271.6 3.2 copy.36
  274.8 5.7 %all-to-all-start.3 = ((bf16[8,160,768]{2,1,0:T(8,128)(2,1)}), bf16[8,160,768]{2,1,0:T(8,128)(2,1)S(1)}, u32[]{:S(2)}, u32[]{:S(2)}) async-start(bf16[8,160,768]{2,1,0:T(8,128)(2,1)} %copy.36), calls=%async_computation.3 | async-start | bytes 3932160 | tf_op jit(solution)/shard_map/all_to_all | solution.py:133
  280.6 0.3 all-reduce.3.cloned.1.call-start
  280.9 2.0 convert_reduce_fusion.1
  282.9 4.6 convolution_bitcast_fusion.1
  287.5 0.0 copy-start.9
  287.6 1.2 convolution_bitcast_fusion
  288.8 1.0 select_maximum_fusion
  289.8 0.0 all-reduce.3.cloned.1.call-update
  289.8 5.6 %fusion.23 = bf16[8,192,640]{2,1,0:T(8,128)(2,1)} fusion(f32[192]{0:T(256)S(1)} %copy-done.9, bf16[8,640,512]{2,1,0:T(8,128)(2,1)} %get-tuple-element.24, bf16[512,192]{0,1:T(8,128)(2,1)S(1)} %copy-done.7), kind=kOutput, calls=%fused_computation.41 | convolution fusion | flops 1008599040 | bytes 7406336 | tf_op jit(solution)/shard_map/lch,hk->lkc/dot_general | solution.py:92
  295.4 136.8 %all-reduce.3.cloned.1.call-done = f32[386,512]{1,0:T(8,128)} async-done(((f32[386,512]{1,0:T(8,128)}), f32[386,512]{1,0:T(8,128)}) %all-reduce.3.cloned.1.call-update) | async-done | bytes 790544 | tf_op jit(solution)/shard_map/psum | solution.py:123
  432.2 1.3 slice.37
  433.5 1.3 slice.39
  434.7 2.0 slice_bitcast_fusion
  436.8 2.4 copy.37
  439.1 4.6 reshape.456
  443.7 2.4 fusion.51
  446.1 3.4 rev.8
  449.5 20.5 %bitcast_convert_fusion = bf16[80,96,1408]{2,1,0:T(8,128)(2,1)} fusion(bf16[80,1,64,1408]{3,2,1,0:T(8,128)(2,1)} %get-tuple-element.7, bf16[80,1,64,1408]{3,2,1,0:T(8,128)(2,1)} %get-tuple-element.6, bf16[80,2,32,96]{3,2,1,0:T(8,128)(2,1)S(1)} %rev.8, bf16[80,2,32,96]{3,2,1,0:T(8,128)(2,1)} %get-tuple-element.8), kind=kOutput, calls=%fused_computation | convolution fusion | flops 2797404160 | bytes 52428800 | tf_op jit(solution)/shard_map/pqlk,pqlj->pkj/dot_general | solution.py:138
  (31 shorter events, 0.1 us)
Async XLA Ops:
  7.2 198.3 %copy-start = (bf16[192,512]{1,0:T(8,128)(2,1)S(1)}, bf16[192,512]{1,0:T(8,128)(2,1)}, u32[]{:S(2)}) copy-start(bf16[192,512]{1,0:T(8,128)(2,1)} %param.11) | copy-start | bytes 589828
  8.3 7.3 %slice-start = ((s8[7208960]{0:T(1024)(128)(4,1)}), s8[4194304]{0:T(1024)(128)(4,1)S(1)}, s32[]{:S(2)}) async-start(s8[7208960]{0:T(1024)(128)(4,1)} %bitcast.95), calls=%async_computation.5 | async-start | bytes 8388608
  8.6 7.1 %slice-start.1 = ((s8[7208960]{0:T(1024)(128)(4,1)}), s8[3014656]{0:T(1024)(128)(4,1)S(1)}, s32[]{:S(2)}) async-start(s8[7208960]{0:T(1024)(128)(4,1)} %bitcast.95), calls=%async_computation.6 | async-start | bytes 6029312
  58.3 13.3 %copy-start.6 = (s32[640]{0:T(1024)S(1)}, s32[640]{0:T(1024)}, u32[]{:S(2)}) copy-start(s32[640]{0:T(1024)} %param.8) | copy-start | bytes 7684
  64.6 66.8 %all-to-all-start = ((bf16[160,8,768]{2,0,1:T(8,128)(2,1)}), bf16[160,8,768]{2,0,1:T(8,128)(2,1)S(1)}, u32[]{:S(2)}, u32[]{:S(2)}) async-start(bf16[160,8,768]{2,0,1:T(8,128)(2,1)} %copy.25), calls=%async_computation | async-start | bytes 3932160 | tf_op jit(solution)/shard_map/all_to_all | solution.py:77
  131.5 1.3 copy-start.1
  192.7 12.8 %copy-start.8 = (f32[512]{0:T(512)S(1)}, f32[512]{0:T(512)}, u32[]{:S(2)}) copy-start(f32[512]{0:T(512)} %param.12) | copy-start | bytes 6148
  205.5 5.6 %copy-start.5 = (bf16[8,48,4,640]{3,1,2,0:T(8,128)(2,1)}, bf16[8,48,4,640]{3,1,2,0:T(8,128)(2,1)S(1)}, u32[]{:S(2)}) copy-start(bf16[8,48,4,640]{3,1,2,0:T(8,128)(2,1)S(1)} %copy.32) | copy-start | bytes 5898244
  205.5 5.5 %copy-start.3 = (bf16[8,192,640]{2,1,0:T(8,128)(2,1)S(1)}, bf16[8,192,640]{2,1,0:T(8,128)(2,1)}, u32[]{:S(2)}) copy-start(bf16[8,192,640]{2,1,0:T(8,128)(2,1)} %param.15) | copy-start | bytes 5898244
  205.5 5.5 %copy-start.7 = (bf16[512,192]{0,1:T(8,128)(2,1)S(1)}, bf16[512,192]{0,1:T(8,128)(2,1)}, u32[]{:S(2)}) copy-start(bf16[512,192]{0,1:T(8,128)(2,1)} %param.13) | copy-start | bytes 589828
  219.7 29.9 %copy-start.2 = (bf16[8,640,512]{2,1,0:T(8,128)(2,1)}, bf16[8,640,512]{2,1,0:T(8,128)(2,1)S(1)}, u32[]{:S(2)}) copy-start(bf16[8,640,512]{2,1,0:T(8,128)(2,1)S(1)} %get-tuple-element.27) | copy-start | bytes 15728644
  274.8 161.9 %all-to-all-start.3 = ((bf16[8,160,768]{2,1,0:T(8,128)(2,1)}), bf16[8,160,768]{2,1,0:T(8,128)(2,1)S(1)}, u32[]{:S(2)}, u32[]{:S(2)}) async-start(bf16[8,160,768]{2,1,0:T(8,128)(2,1)} %copy.36), calls=%async_computation.3 | async-start | bytes 3932160 | tf_op jit(solution)/shard_map/all_to_all | solution.py:133
  280.6 151.6 %all-reduce.3.cloned.1.call-start = ((), (), s32[]{:S(2)}) async-start(), calls=%async_computation.4 | async-start | bytes 1605632 | tf_op jit(solution)/shard_map/psum | solution.py:123
  280.9 6.7 %copy-start.4 = (bf16[8,192,640]{2,1,0:T(8,128)(2,1)S(1)}, bf16[8,192,640]{2,1,0:T(8,128)(2,1)}, u32[]{:S(2)}) copy-start(bf16[8,192,640]{2,1,0:T(8,128)(2,1)} %param.15) | copy-start | bytes 5898244
  280.9 6.7 %slice-start.2 = ((s8[5242880]{0:T(1024)(128)(4,1)}), s8[4194304]{0:T(1024)(128)(4,1)S(1)}, s32[]{:S(2)}) async-start(s8[5242880]{0:T(1024)(128)(4,1)} %bitcast.110), calls=%async_computation.7 | async-start | bytes 8388608
  282.9 4.6 slice-start.3
  287.5 2.3 copy-start.9
Sparse Core Ops, SparseCore 0:
  289.9 142.2 all-reduce.2
where the time goes:
time: 484 us; the launch traced here: 477 us
  waiting for transfers between devices  137 us (28%)
  local copies, waits for them, and re-layouts  113 us (23%)
  matrix products  85.8 us (18%)
  other arithmetic  59.6 us (12%)
  blocking collectives  54.4 us (11%)
  between operations  14.7 us (3%)
  starting transfers between devices  12.9 us (3%)
    psum x1, waiting for transfers between devices, per_device(): summed = lax.psum(stacked, ('lat', 'lon'))  137 us
    all_to_all x1, blocking collectives, per_device(): lax.all_to_all(all_columns, 'lon', split_axis=2, concat_axis=1, tiled=True)  27.4 us
    all_to_all x1, blocking collectives, per_device(): lax.all_to_all(grid_grad, 'lon', split_axis=1, concat_axis=2, tiled=True)  26.9 us
    dot_general x1, matrix products, per_device(): jnp.einsum('pqlk,pqlj->pkj', pair_grad, basis, preferred_element_type=jnp...  20.5 us
    dot_general x1, matrix products, per_device(): jnp.einsum('pqlj,pkj->pqlk', basis, spectral, preferred_element_type=jnp....  20 us
    unnamed x30, local copies, waits for them, and re-layouts  17.3 us
    select_n x1, other arithmetic, per_device(): jnp.where(lower_part[:, None, :], rows, zero)  14.2 us
    add x1, local copies, waits for them, and re-layouts, fourier_table(): sin_a[:, :, None] * cos_b[:, None, :]  14 us
  transfers between devices with their start and end apart: 3, of which 1 were waited for; matrix products, arithmetic and copies ran while one was open for 17% of the time, Pallas kernels for 0%

commit v1 on v0

--- a/solution.py
+++ b/solution.py
@@ -120,7 +120,7 @@
         ],
         axis=0,
     )
-    summed = lax.psum(stacked, ("lat", "lon"))
+    summed = jnp.sum(lax.all_gather(stacked, ("lat", "lon")), axis=0)
     in_weight_grad = summed[:channels, :hid]
     out_weight_grad = summed[channels : 2 * channels, :hid].T
     in_bias_grad = summed[2 * channels, :hid]

time: 484 us -> 446 us (0.921)
  waiting for transfers between devices: 137 us -> 106 us
  blocking collectives: 54.4 us -> 32.5 us
  other arithmetic: 59.6 us -> 69.5 us
  starting transfers between devices: 12.9 us -> 17.9 us
    psum x1 -> x0, waiting for transfers between devices: 137 us -> none  [per_device(): summed = lax.psum(stacked, ('lat', 'lon'))]
    all_to_all x1, waiting for transfers between devices: 0.01 us -> 75 us  [per_device(): lax.all_to_all(flat_grad, 'lat', split_axis=0, concat_axis=1, tiled=True)]
    all_to_all x1 -> x0, blocking collectives: 27.4 us -> none  [per_device(): lax.all_to_all(all_columns, 'lon', split_axis=2, concat_axis=1, tiled=True)]
    all_to_all x0 -> x1, waiting for transfers between devices: none -> 21.5 us  [per_device(): lax.all_to_all(all_columns, 'lon', split_axis=2, concat_axis=1, tiled=True)]
    reduce_sum x0 -> x1, other arithmetic: none -> 10.1 us  [per_device(): summed = jnp.sum(lax.all_gather(stacked, ('lat', 'lon')), axis=0)]
    all_gather x0 -> x1, waiting for transfers between devices: none -> 9.89 us  [per_device(): summed = jnp.sum(lax.all_gather(stacked, ('lat', 'lon')), axis=0)]
    all_to_all x1, blocking collectives: 26.9 us -> 32.5 us  [per_device(): lax.all_to_all(grid_grad, 'lon', split_axis=1, concat_axis=2, tiled=True)]
    unnamed x30 -> x24, local copies, waits for them, and re-layouts: 17.3 us -> 20.6 us
  transfers between devices with their start and end apart: 3 -> 4, of which waited for: 1 -> 3; matrix products, arithmetic and copies ran while one was open for 17% -> 28% of each run, Pallas kernels for 0% -> 0%
where the time goes in v1:
time: 446 us; the launch traced here: 438 us
  local copies, waits for them, and re-layouts  114 us (26%)
  waiting for transfers between devices  106 us (24%)
  matrix products  83.4 us (19%)
  other arithmetic  69.5 us (16%)
  blocking collectives  32.5 us (7%)
  starting transfers between devices  17.9 us (4%)
  between operations  14.8 us (3%)
    all_to_all x1, waiting for transfers between devices, per_device(): lax.all_to_all(flat_grad, 'lat', split_axis=0, concat_axis=1, tiled=True)  75 us
    all_to_all x1, blocking collectives, per_device(): lax.all_to_all(grid_grad, 'lon', split_axis=1, concat_axis=2, tiled=True)  32.5 us
    all_to_all x1, waiting for transfers between devices, per_device(): lax.all_to_all(all_columns, 'lon', split_axis=2, concat_axis=1, tiled=True)  21.5 us
    dot_general x1, matrix products, per_device(): jnp.einsum('pqlk,pqlj->pkj', pair_grad, basis, preferred_element_type=jnp...  20.7 us
    unnamed x24, local copies, waits for them, and re-layouts  20.6 us
    dot_general x1, matrix products, per_device(): jnp.einsum('pqlj,pkj->pqlk', basis, spectral, preferred_element_type=jnp....  20 us
    select_n x1, other arithmetic, per_device(): jnp.where(lower_part[:, None, :], rows, zero)  14.1 us
    sub x1, local copies, waits for them, and re-layouts, fourier_table(): cos_a[:, :, None] * cos_b[:, None, :]  14 us
  transfers between devices with their start and end apart: 4, of which 3 were waited for; matrix products, arithmetic and copies ran while one was open for 28% of the time, Pallas kernels for 0%

profile of v1, /device:TPU:1, one launch (start us, length us, event | category | flops | bytes accessed | tf_op | source)
XLA Modules:
  0.0 438.4 jit_solution(5686833686874475718)
XLA Ops:
  7.2 0.0 copy-start
  7.2 0.8 dynamic-slice_subtract_fusion
  8.0 0.3 select_convert_fusion
  8.3 0.0 slice-start
  8.4 0.2 iota_compare_fusion.2
  8.6 0.0 slice-start.1
  8.6 7.1 %multiply_bitcast_fusion = bf16[80,1,32,1408]{3,2,1,0:T(8,128)(2,1)} fusion(bf16[80,32,1408]{2,1,0:T(8,128)(2,1)} %param.10, bf16[80,1408]{1,0:T(8,128)(2,1)S(1)} %select_convert_fusion), kind=kLoop, calls=%fused_computation.25 | loop fusion | flops 3604480 | bytes 14643200 | tf_op jit(solution)/shard_map/concatenate | solution.py:60
  15.7 14.1 %broadcast_select_fusion.1 = (bf16[80,1,64,1408]{3,2,1,0:T(8,128)(2,1)}, bf16[80,1,64,1408]{3,2,1,0:T(8,128)(2,1)}) fusion(pred[80,1408]{1,0:T(8,128)(4,1)S(1)} %get-tuple-element.22, bf16[80,1,32,1408]{3,2,1,0:T(8,128)(2,1)} %multiply_bitcast_fusion, bf16[80,1,32,1408]{3,2,1,0:T(8,128)(2,1)S(1)} %bitcast.99, pred[80,1408]{1,0:T(8,128)(4,1)S(1)} %get-tuple-element.23), kind=kLoop, calls=%fused_computation.8 | loop fusion | flops 43253760 | bytes 43479040 | tf_op jit(solution)/shard_map/jit(_where)/select_n | solution.py:64
  29.8 20.0 %fusion.18 = bf16[80,2,64,96]{3,2,1,0:T(8,128)(2,1)} fusion(bf16[80,96,1408]{2,1,0:T(8,128)(2,1)} %param.9, bf16[80,1,64,1408]{3,2,1,0:T(8,128)(2,1)} %get-tuple-element.7, bf16[80,1,64,1408]{3,2,1,0:T(8,128)(2,1)} %get-tuple-element.6), kind=kOutput, calls=%fused_computation.36 | convolution fusion | flops 2783641600 | bytes 52428800 | tf_op jit(solution)/shard_map/pqlj,pkj->pqlk/dot_general | solution.py:70
  49.8 3.4 fusion.53
  53.1 2.6 rev.7
  55.7 2.5 pad_maximum_fusion.4
  58.2 3.1 all_to_all.50
  61.4 3.2 copy.25
  64.6 6.9 %all-to-all-start = ((bf16[160,8,768]{2,0,1:T(8,128)(2,1)}), bf16[160,8,768]{2,0,1:T(8,128)(2,1)S(1)}, u32[]{:S(2)}, u32[]{:S(2)}) async-start(bf16[160,8,768]{2,0,1:T(8,128)(2,1)} %copy.25), calls=%async_computation | async-start | bytes 3932160 | tf_op jit(solution)/shard_map/all_to_all | solution.py:77
  71.6 0.2 copy.27
  71.8 0.2 reshape.455
  72.0 2.6 fusion.30
  74.6 1.3 fusion.45
  75.9 13.6 %multiply_subtract_fusion = (f32[1280,20,128]{0,2,1:T(8,128)}, f32[1280,20,128]{0,2,1:T(8,128)}) fusion(f32[1280,128]{0,1:T(8,128)S(1)} %get-tuple-element.21, f32[1280,20]{0,1:T(8,128)} %get-tuple-element.17, f32[1280,128]{0,1:T(8,128)S(1)} %get-tuple-element.20, f32[1280,20]{0,1:T(8,128)} %get-tuple-element.16), kind=kLoop, calls=%fused_computation.13 | loop fusion | flops 19660800 | bytes 27729920 | tf_op jit(solution)/shard_map/sub | solution.py:38
  89.5 13.9 %copy.29 = f32[1280,1,2560]{2,0,1:T(8,128)} copy(f32[1280,1,2560]{0,2,1:T(8,128)} %bitcast.96) | data formatting | bytes 26214400 | tf_op jit(solution)/shard_map/add | solution.py:39
  103.5 14.0 %copy.28 = f32[1280,1,2560]{2,0,1:T(8,128)} copy(f32[1280,1,2560]{0,2,1:T(8,128)} %bitcast.95) | data formatting | bytes 26214400 | tf_op jit(solution)/shard_map/sub | solution.py:38
  117.5 13.9 %multiply_convert_fusion = (bf16[1280,1,2560]{2,0,1:T(8,128)(2,1)}, bf16[1280,1,2560]{2,0,1:T(8,128)(2,1)}) fusion(f32[1280,1,2560]{2,0,1:T(8,128)} %copy.29, f32[1280]{0:T(1024)S(1)} %get-tuple-element.19, f32[1280,1,2560]{2,0,1:T(8,128)} %copy.28, f32[1280]{0:T(1024)S(1)} %get-tuple-element.18), kind=kLoop, calls=%fused_computation.10 | loop fusion | flops 13107200 | bytes 39331840 | tf_op jit(solution)/shard_map/convert.1
  131.4 1.3 copy-done.1
  132.7 4.1 copy.26
  136.7 5.2 %reshape.454 = bf16[1280,8,48,2]{0,3,2,1:T(2,128)(2,1)} reshape(bf16[8,160,768]{1,0,2:T(8,128)(2,1)S(1)} %copy.26) | data formatting | bytes 3932160 | tf_op jit(solution)/shard_map/reshape | solution.py:79
  142.0 8.9 %fusion.12 = bf16[8,48,2560]{2,1,0:T(8,128)(2,1)S(1)} fusion(bf16[1280,1,2560]{2,0,1:T(8,128)(2,1)} %get-tuple-element.28, bf16[1280,1,2560]{2,0,1:T(8,128)(2,1)} %get-tuple-element.29, bf16[1280,8,48,2]{0,3,2,1:T(2,128)(2,1)} %reshape.454), kind=kOutput, calls=%fused_computation.27 | convolution fusion | flops 5040701440 | bytes 17039360 | tf_op jit(solution)/shard_map/glkc,gcn->lkn/dot_general | solution.py:82
  150.9 5.4 %copy.31 = bf16[8,48,2560]{1,0,2:T(8,128)(2,1)} copy(bf16[8,48,2560]{2,1,0:T(8,128)(2,1)S(1)} %fusion.12) | data formatting | bytes 3932160 | tf_op jit(solution)/shard_map/convert_element_type | solution.py:84
  156.3 9.6 %reshape.471 = bf16[4,2,122880]{2,1,0:T(2,128)(2,1)} reshape(bf16[2560,8,48]{2,1,0:T(8,128)(2,1)} %bitcast.100) | data formatting | bytes 3932160
  165.9 4.5 %all-to-all-start.1 = ((bf16[4,2,122880]{2,1,0:T(2,128)(2,1)}), bf16[4,2,122880]{2,1,0:T(2,128)(2,1)S(1)}, u32[]{:S(2)}, u32[]{:S(2)}) async-start(bf16[4,2,122880]{2,1,0:T(2,128)(2,1)} %reshape.471), calls=%async_computation.1 | async-start | bytes 3932160 | tf_op jit(solution)/shard_map/all_to_all | solution.py:85
  170.4 1.9 convert_reduce_fusion.1
  172.3 21.5 %all-to-all-done.1 = bf16[4,2,122880]{2,1,0:T(2,128)(2,1)S(1)} async-done(((bf16[4,2,122880]{2,1,0:T(2,128)(2,1)}), bf16[4,2,122880]{2,1,0:T(2,128)(2,1)S(1)}, u32[]{:S(2)}, u32[]{:S(2)}) %all-to-all-start.1) | async-done | bytes 1966112 | tf_op jit(solution)/shard_map/all_to_all | solution.py:85
  193.9 6.3 %reshape.472 = bf16[2560,8,48]{2,1,0:T(8,128)(2,1)} reshape(bf16[4,2,122880]{2,1,0:T(2,128)(2,1)S(1)} %all-to-all-done.1) | data formatting | bytes 3932160
  200.1 5.7 %copy.32 = bf16[8,48,4,640]{3,1,2,0:T(8,128)(2,1)S(1)} copy(bf16[8,48,4,640]{1,0,3,2:T(8,128)(2,1)} %bitcast.101) | data formatting | bytes 3932160 | tf_op jit(solution)/shard_map/all_to_all | solution.py:85
  205.9 3.8 multiply_convert_fusion.2
  209.7 1.2 convolution_bitcast_fusion
  210.9 1.1 copy-done.8
  212.0 8.7 %convert_reduce_fusion = (f32[512]{0:T(512)S(1)}, bf16[8,640,512]{2,1,0:T(8,128)(2,1)S(1)}) fusion(f32[8,640,512]{2,1,0:T(8,128)S(1)} %get-tuple-element.25, f32[512]{0:T(512)S(1)} %copy-done.6, bf16[8,192,640]{2,1,0:T(8,128)(2,1)S(1)} %copy-done.3, bf16[512,192]{0,1:T(8,128)(2,1)S(1)} %copy-done.5), kind=kOutput, calls=%fused_computation.21 | convolution fusion | flops 1066925568 | bytes 17895424 | tf_op jit(solution)/shard_map/lkc,hk->lch/dot_general | solution.py:99
  220.7 2.4 copy-done.2
  223.1 1.2 convolution_bitcast_fusion.1
  224.2 0.9 fusion.24
  225.2 0.0 all-gather.4.cloned.1.call-update
  225.2 4.3 convert_bitcast_fusion
  229.5 1.1 copy.33
  230.7 32.5 %all_to_all.68 = bf16[8,192,640]{2,0,1:T(8,128)(2,1)S(1)} all-to-all(bf16[8,192,640]{2,0,1:T(8,128)(2,1)S(1)} %copy.33), channel_id=1, replica_groups=mesh['lat'=8,'lon'=4] {'lon'}, dimensions={1} | all-to-all | bytes 3932160 | tf_op jit(solution)/shard_map/all_to_all | solution.py:128
  263.2 1.5 copy.45
  264.7 2.2 reshape.466
  266.9 9.0 %fusion.14 = bf16[1280,8,48,2]{0,2,3,1:T(8,128)(2,1)S(1)} fusion(bf16[1280,1,2560]{2,0,1:T(8,128)(2,1)} %get-tuple-element.28, bf16[1280,1,2560]{2,0,1:T(8,128)(2,1)} %get-tuple-element.29, bf16[8,48,2560,1]{2,1,0,3:T(8,128)(2,1)} %reshape.466), kind=kOutput, calls=%fused_computation.31 | convolution fusion | flops 5060362240 | bytes 17039360 | tf_op jit(solution)/shard_map/gcn,lkn->glkc/dot_general | solution.py:129
  275.9 2.8 copy.35
  278.7 6.4 %all_to_all.61 = bf16[8,160,768]{1,0,2:T(8,128)(2,1)S(1)} reshape(bf16[1280,8,48,2]{0,3,2,1:T(2,128)(2,1)} %copy.35) | data formatting | bytes 3932160 | tf_op jit(solution)/shard_map/all_to_all | solution.py:133
  285.1 3.2 copy.36
  288.4 6.5 %all-to-all-start.3 = ((bf16[8,160,768]{2,1,0:T(8,128)(2,1)}), bf16[8,160,768]{2,1,0:T(8,128)(2,1)S(1)}, u32[]{:S(2)}, u32[]{:S(2)}) async-start(bf16[8,160,768]{2,1,0:T(8,128)(2,1)} %copy.36), calls=%async_computation.3 | async-start | bytes 3932160 | tf_op jit(solution)/shard_map/all_to_all | solution.py:133
  294.9 5.6 %fusion.23 = bf16[8,192,640]{2,1,0:T(8,128)(2,1)} fusion(f32[192]{0:T(256)S(1)} %copy-done.7, bf16[8,640,512]{2,1,0:T(8,128)(2,1)} %copy-done.8, bf16[512,192]{0,1:T(8,128)(2,1)S(1)} %copy-done.5), kind=kOutput, calls=%fused_computation.41 | convolution fusion | flops 1008599040 | bytes 7406336 | tf_op jit(solution)/shard_map/lch,hk->lkc/dot_general | solution.py:92
  300.5 75.0 %all-to-all-done.3 = bf16[8,160,768]{2,1,0:T(8,128)(2,1)S(1)} async-done(((bf16[8,160,768]{2,1,0:T(8,128)(2,1)}), bf16[8,160,768]{2,1,0:T(8,128)(2,1)S(1)}, u32[]{:S(2)}, u32[]{:S(2)}) %all-to-all-start.3) | async-done | bytes 1966112 | tf_op jit(solution)/shard_map/all_to_all | solution.py:133
  375.5 2.4 copy.37
  377.9 4.6 %reshape.456 = bf16[80,2,64,96]{3,2,1,0:T(8,128)(2,1)S(1)} reshape(bf16[160,8,768]{2,1,0:T(8,128)(2,1)} %copy.37) | data formatting | bytes 3932160 | tf_op jit(solution)/shard_map/reshape | solution.py:134
  382.5 2.4 fusion.52
  384.8 3.5 rev.8
  388.3 20.7 %bitcast_convert_fusion = bf16[80,96,1408]{2,1,0:T(8,128)(2,1)} fusion(bf16[80,1,64,1408]{3,2,1,0:T(8,128)(2,1)} %get-tuple-element.7, bf16[80,1,64,1408]{3,2,1,0:T(8,128)(2,1)} %get-tuple-element.6, bf16[80,2,32,96]{3,2,1,0:T(8,128)(2,1)S(1)} %rev.8, bf16[80,2,32,96]{3,2,1,0:T(8,128)(2,1)} %get-tuple-element.8), kind=kOutput, calls=%fused_computation | convolution fusion | flops 2797404160 | bytes 52428800 | tf_op jit(solution)/shard_map/pqlk,pqlj->pkj/dot_general | solution.py:138
  409.0 9.9 %all-gather.4.cloned.1.call-done = f32[32,386,512]{2,1,0:T(8,128)} async-done(((f32[1,386,512]{2,1,0:T(8,128)}), f32[32,386,512]{2,1,0:T(8,128)}) %all-gather.4.cloned.1.call-update) | async-done | bytes 25296912 | tf_op jit(solution)/shard_map/all_gather | solution.py:123
  418.9 10.1 %reduce_sum.29 = f32[386,512]{1,0:T(8,128)S(1)} reduce(f32[32,386,512]{2,1,0:T(8,128)} %all-gather.4.cloned.1.call-done, f32[]{:T(128)} %constant.77.clone.1), dimensions={0}, to_apply=%region_2.3 | reduce | flops 6126592 | bytes 26087428 | tf_op jit(solution)/shard_map/reduce_sum | solution.py:123
  429.1 0.9 slice_bitcast_fusion
  430.0 0.6 slice.37
  430.6 0.6 slice.39
  (26 shorter events, 0.1 us)
Async XLA Ops:
  7.2 198.7 %copy-start = (bf16[192,512]{1,0:T(8,128)(2,1)S(1)}, bf16[192,512]{1,0:T(8,128)(2,1)}, u32[]{:S(2)}) copy-start(bf16[192,512]{1,0:T(8,128)(2,1)} %param.11) | copy-start | bytes 589828
  8.3 7.3 %slice-start = ((s8[7208960]{0:T(1024)(128)(4,1)}), s8[4194304]{0:T(1024)(128)(4,1)S(1)}, s32[]{:S(2)}) async-start(s8[7208960]{0:T(1024)(128)(4,1)} %bitcast.97), calls=%async_computation.5 | async-start | bytes 8388608
  8.6 7.1 %slice-start.1 = ((s8[7208960]{0:T(1024)(128)(4,1)}), s8[3014656]{0:T(1024)(128)(4,1)S(1)}, s32[]{:S(2)}) async-start(s8[7208960]{0:T(1024)(128)(4,1)} %bitcast.97), calls=%async_computation.6 | async-start | bytes 6029312
  58.2 13.3 %copy-start.4 = (s32[640]{0:T(1024)S(1)}, s32[640]{0:T(1024)}, u32[]{:S(2)}) copy-start(s32[640]{0:T(1024)} %param.8) | copy-start | bytes 7684
  64.6 66.8 %all-to-all-start = ((bf16[160,8,768]{2,0,1:T(8,128)(2,1)}), bf16[160,8,768]{2,0,1:T(8,128)(2,1)S(1)}, u32[]{:S(2)}, u32[]{:S(2)}) async-start(bf16[160,8,768]{2,0,1:T(8,128)(2,1)} %copy.25), calls=%async_computation | async-start | bytes 3932160 | tf_op jit(solution)/shard_map/all_to_all | solution.py:77
  131.4 1.3 copy-start.1
  165.9 28.0 %all-to-all-start.1 = ((bf16[4,2,122880]{2,1,0:T(2,128)(2,1)}), bf16[4,2,122880]{2,1,0:T(2,128)(2,1)S(1)}, u32[]{:S(2)}, u32[]{:S(2)}) async-start(bf16[4,2,122880]{2,1,0:T(2,128)(2,1)} %reshape.471), calls=%async_computation.1 | async-start | bytes 3932160 | tf_op jit(solution)/shard_map/all_to_all | solution.py:85
  170.4 248.5 %all-gather.4.cloned.1.call-start = ((), (), s32[]{:S(2)}) async-start(), calls=%async_computation.4 | async-start | bytes 26492928 | tf_op jit(solution)/shard_map/all_gather | solution.py:123
  172.3 33.5 %copy-start.6 = (f32[512]{0:T(512)S(1)}, f32[512]{0:T(512)}, u32[]{:S(2)}) copy-start(f32[512]{0:T(512)} %param.12) | copy-start | bytes 6148
  205.9 3.9 copy-start.3
  209.7 2.3 copy-start.8
  209.7 2.3 copy-start.5
  220.7 2.4 copy-start.2
  278.7 16.2 %copy-start.7 = (f32[192]{0:T(256)S(1)}, f32[192]{0:T(256)}, u32[]{:S(2)}) copy-start(f32[192]{0:T(256)} %param.14) | copy-start | bytes 2308
  288.4 87.2 %all-to-all-start.3 = ((bf16[8,160,768]{2,1,0:T(8,128)(2,1)}), bf16[8,160,768]{2,1,0:T(8,128)(2,1)S(1)}, u32[]{:S(2)}, u32[]{:S(2)}) async-start(bf16[8,160,768]{2,1,0:T(8,128)(2,1)} %copy.36), calls=%async_computation.3 | async-start | bytes 3932160 | tf_op jit(solution)/shard_map/all_to_all | solution.py:133
Sparse Core Ops, SparseCore 0:
  225.3 193.5 all-gather.3
